TPU v7x, 32 devices: a whole 2x2x4 slice. The times are simulated.
32 devices in a mesh: scene: 2 (over y), tok: 8 (over z, x), hid: 2 (over core).
Axes of the slice: x: 2, y: 2, z: 4, core: 2. Of those that a mesh axis runs over, the one named last changes fastest.
Arguments:
- input_keys: bfloat16 [16384, 384], P(('scene', 'tok'), 'hid'), parts along dimension 0, may hold values from -6 to 6
- input_values: bfloat16 [16384, 384], P(('scene', 'tok'), 'hid'), parts along dimension 0, may hold values from -6 to 6
- input_lr: float32 [16384], P(('scene', 'tok')), parts along dimension 0, may hold values from 0.1 to 1
- gate_weight: bfloat16 [384, 1536], P('tok', 'hid'), may hold values from -0.3125 to 0.3125
- up_weight: bfloat16 [384, 1536], P('tok', 'hid'), may hold values from -0.3125 to 0.3125
- down_weight: bfloat16 [384, 1536], P('tok', 'hid'), may hold values from -0.15625 to 0.15625
- queries: bfloat16 [2048, 384], P(('scene', 'tok'), 'hid'), parts along dimension 0, may hold values from -6 to 6
- out_grad: bfloat16 [2048, 384], P(('scene', 'tok'), 'hid'), parts along dimension 0, may hold values from -6 to 6
Outputs:
- target_out: bfloat16 [2048, 384], P(('scene', 'tok'), 'hid'), parts along dimension 0
- query_grad: bfloat16 [2048, 384], P(('scene', 'tok'), 'hid'), parts along dimension 0
There are 2 independent parts, one for each index of `scene`. A program takes and returns all parts, laid end to end along the dimension named above; an argument that names none is the same for every part. Nothing has to cross between parts.
All inputs are finite; a program needn't handle non-finite values.
Results may differ from a plain program's by a relative error of at most 0.009.
Values may be sent and summed in bfloat16 or wider, within the bound.
A program may use at most 64 MiB of HBM per device.

v0:
```python
import jax
import jax.numpy as jnp
from jax import lax
from jax.sharding import PartitionSpec as P

HID = 1536


step_ratio = 0.5
epsilon = 1e-06


def silu_slope(pre):
    sigma = jax.nn.sigmoid(pre)
    return sigma * (1.0 + pre * (1.0 - sigma))


def contract_rows(left, right):
    return lax.dot_general(
        left, right, (((0,), (0,)), ((), ())), preferred_element_type=jnp.float32
    )


def contract_cols(left, right):
    return lax.dot_general(
        left, right, (((1,), (1,)), ((), ())), preferred_element_type=jnp.float32
    )


def finish(moved, wsq, msq):
    return (moved * (jnp.sqrt(wsq) / jnp.sqrt(msq + epsilon))[:, None]).astype(jnp.bfloat16)


def shards(
    input_keys, input_values, input_lr, gate_weight, up_weight, down_weight, queries, out_grad
):
    keys, values = (
        lax.all_gather(input_keys, "hid", axis=1, tiled=True),
        lax.all_gather(input_values, "hid", axis=1, tiled=True),
    )
    w_gate, w_up, w_down = (
        lax.all_gather(gate_weight, "tok", axis=0, tiled=True),
        lax.all_gather(up_weight, "tok", axis=0, tiled=True),
        lax.all_gather(down_weight, "tok", axis=0, tiled=True),
    )
    scaled = (input_lr[:, None] * values.astype(jnp.float32)).astype(jnp.bfloat16)
    key_gate = jnp.dot(keys, w_gate, preferred_element_type=jnp.float32)
    key_up = jnp.dot(keys, w_up, preferred_element_type=jnp.float32)
    gate_act = jax.nn.silu(key_gate)
    key_act = (gate_act * key_up).astype(jnp.bfloat16)
    back = jnp.dot(scaled, w_down, preferred_element_type=jnp.float32)
    d_gate = (-back * key_up * silu_slope(key_gate)).astype(jnp.bfloat16)
    d_up = (-back * gate_act).astype(jnp.bfloat16)
    width = gate_weight.shape[1]
    grads = lax.psum(
        jnp.concatenate(
            [
                contract_rows(keys, d_gate),
                contract_rows(keys, d_up),
                -contract_rows(scaled, key_act),
            ],
            axis=1,
        ),
        "tok",
    )
    olds = (w_gate, w_up, w_down)
    pieces = [grads[:, :width], grads[:, width : 2 * width], grads[:, 2 * width :]]
    weights = [old.astype(jnp.float32) for old in olds]
    renewed = []
    stats = []
    for weight, grad in zip(weights, pieces):
        stats.append(jnp.sum(weight * weight, axis=1))
        stats.append(jnp.sum(weight * grad, axis=1))
        stats.append(jnp.sum(grad * grad, axis=1))
    totals = lax.psum(
        (stats[0], stats[1], stats[2], stats[3], stats[4], stats[5], stats[6], stats[7], stats[8]),
        "hid",
    )
    for index in range(3):
        wsq = totals[3 * index] / HID
        cross = totals[3 * index + 1] / HID
        gsq = totals[3 * index + 2] / HID
        scale = step_ratio * jnp.sqrt(wsq) / jnp.sqrt(gsq + epsilon)
        moved = weights[index] - scale[:, None] * pieces[index]
        msq = wsq - 2.0 * scale * cross + scale * scale * gsq
        renewed.append(finish(moved, wsq, msq))
    new_gate, new_up, new_down = (renewed[0], renewed[1], renewed[2])
    query_rows, grad_rows = (
        lax.all_gather(queries, "hid", axis=1, tiled=True),
        lax.all_gather(out_grad, "hid", axis=1, tiled=True),
    )
    query_gate = jnp.dot(query_rows, new_gate, preferred_element_type=jnp.float32)
    query_up = jnp.dot(query_rows, new_up, preferred_element_type=jnp.float32)
    query_silu = jax.nn.silu(query_gate)
    query_act = (query_silu * query_up).astype(jnp.bfloat16)
    out_part = contract_cols(query_act, new_down)
    query_back = jnp.dot(grad_rows, new_down, preferred_element_type=jnp.float32)
    q_gate_grad = (query_back * query_up * silu_slope(query_gate)).astype(jnp.bfloat16)
    q_up_grad = (query_back * query_silu).astype(jnp.bfloat16)
    grad_part = contract_cols(q_gate_grad, new_gate) + contract_cols(q_up_grad, new_up)
    out_sum, grad_sum = (
        lax.psum_scatter(
            out_part.astype(jnp.bfloat16), "hid", scatter_dimension=1, tiled=True
        ).astype(jnp.float32),
        lax.psum_scatter(
            grad_part.astype(jnp.bfloat16), "hid", scatter_dimension=1, tiled=True
        ).astype(jnp.float32),
    )
    return (out_sum.astype(jnp.bfloat16), grad_sum.astype(jnp.bfloat16))


def solution(mesh):
    return jax.shard_map(
        shards,
        mesh=mesh,
        in_specs=(
            P(("scene", "tok"), "hid"),
            P(("scene", "tok"), "hid"),
            P(("scene", "tok")),
            P("tok", "hid"),
            P("tok", "hid"),
            P("tok", "hid"),
            P(("scene", "tok"), "hid"),
            P(("scene", "tok"), "hid"),
        ),
        out_specs=(P(("scene", "tok"), "hid"), P(("scene", "tok"), "hid")),
        check_vma=False,
    )
```

profile of v0, /device:TPU:0, one launch (start us, length us, event | category | flops | bytes accessed | tf_op | source)
XLA Modules:
  0.0 297.7 jit_solution(15559393787212214560)
XLA Ops:
  7.2 0.0 copy-start.6
  7.2 0.0 all-reduce.3.cloned.1.call-start
  7.2 2.7 all_gather.24
  9.9 33.4 %all_gather.21 = bf16[384,768]{1,0:T(8,128)(2,1)S(1)} all-gather(bf16[48,768]{1,0:T(8,128)(2,1)} %param.11), channel_id=1, replica_groups=mesh['scene'=2,'tok'=8,'hid'=2] {'tok'}, dimensions={0}, use_global_device_ids=true | all-gather | bytes 663552 | tf_op jit(solution)/shard_map/all_gather | solution.py:42
  43.4 0.0 copy-done.6
  43.4 31.3 %all_gather.25 = bf16[384,768]{1,0:T(8,128)(2,1)S(1)} all-gather(bf16[48,768]{1,0:T(8,128)(2,1)S(1)} %copy-done.6), channel_id=1, replica_groups=mesh['scene'=2,'tok'=8,'hid'=2] {'tok'}, dimensions={0}, use_global_device_ids=true | all-gather | bytes 663552 | tf_op jit(solution)/shard_map/all_gather | solution.py:43
  74.6 1.0 fusion.34
  75.7 0.0 copy-start.5
  75.7 0.0 copy-start.7
  75.7 1.0 fusion.33
  76.7 0.0 copy-done.5
  76.7 0.0 copy-start.10
  76.7 2.4 all_gather.22
  79.1 0.0 copy-done.7
  79.1 31.4 %all_gather.23 = bf16[384,768]{1,0:T(8,128)(2,1)S(1)} all-gather(bf16[48,768]{1,0:T(8,128)(2,1)S(1)} %copy-done.7), channel_id=1, replica_groups=mesh['scene'=2,'tok'=8,'hid'=2] {'tok'}, dimensions={0}, use_global_device_ids=true | all-gather | bytes 663552 | tf_op jit(solution)/shard_map/all_gather | solution.py:44
  110.5 0.0 copy-done.10
  110.5 1.0 fusion.20
  111.6 1.2 fusion.6
  112.8 1.5 fusion.4
  114.3 1.3 fusion.5
  115.6 2.0 pad_maximum_fusion
  117.6 0.0 all-reduce.3.cloned.1.call-update
  117.7 0.0 copy-start.8
  117.7 0.0 copy-start.9
  117.7 0.0 reduce-scatter.5.cloned.1.call-start
  117.7 1.1 copy.14
  118.8 1.1 copy.16
  119.8 1.1 copy.17
  121.0 0.0 copy-done.8
  121.0 2.0 all_gather.27
  123.0 0.0 copy-done.9
  123.0 2.0 all_gather.26
  125.0 132.9 %all-reduce.3.cloned.1.call-done = f32[384,2304]{0,1:T(8,128)} async-done(((f32[384,2304]{0,1:T(8,128)}), f32[384,2304]{0,1:T(8,128)}) %all-reduce.3.cloned.1.call-update) | async-done | bytes 3538960 | tf_op jit(solution)/shard_map/psum | solution.py:55
  257.8 0.0 copy-start
  257.9 4.1 %multiply_reduce_fusion.2 = (f32[384]{0:T(512)S(1)}, f32[384]{0:T(512)S(1)}, f32[384]{0:T(512)S(1)}, f32[384]{0:T(512)S(1)}, f32[384]{0:T(512)}, /*index=5*/f32[...) fusion(f32[384,2304]{0,1:T(8,128)} %all-reduce.3.cloned.1.call-done, bf16[384,768]{0,1:T(8,128)(2,1)} %copy.14, ...), kind=kLoop, calls=%fused_computation.39 | loop fusion | flops 6189696 | bytes 5322240 | tf_op jit(solution)/shard_map/reduce_sum | solution.py:74
  261.9 4.6 %all-reduce = (f32[384]{0:T(512)}, f32[384]{0:T(512)}, f32[384]{0:T(512)}, f32[384]{0:T(512)}, f32[384]{0:T(512)}, /*index=5*/f32[384]{0:T(512)}, f32[384]{0:T(512)}, f32[384]{0:T(512)}, f32[384]{0:T(512)}) all-reduce(f32[384]{0:T(512)S(1)} %get-tuple-element.5, ...), channel_id=1, replica_groups=mesh['scene'=2,'tok'=8,'hid'=2] {'hid'}, use_global_device_ids=true, to_apply=%region_18.19 | all-reduce | flops 3456 | bytes 27648 | tf_op jit(solution)/shard_map/psum | solution.py:75
  266.5 0.7 rsqrt_multiply_fusion.5
  267.2 0.8 rsqrt_multiply_fusion.1
  268.0 0.0 copy-done
  268.0 0.0 copy-start.3
  268.0 2.0 fusion.9
  270.0 0.0 copy-start.1
  270.1 0.0 copy-start.4
  270.1 0.0 copy-done.3
  270.1 0.3 convolution_bitcast_fusion.1
  270.4 0.3 convolution_bitcast_fusion.2
  270.7 0.3 copy-done.4
  271.0 0.3 convolution_bitcast_fusion
  271.4 0.0 copy-done.1
  271.4 0.5 fusion.24
  271.8 0.0 copy-start.2
  271.8 1.1 fusion.19
  272.9 0.0 reduce-scatter.5.cloned.1.call-update
  272.9 0.0 reduce-scatter.3.cloned.1.call-start
  273.0 0.0 copy-done.2
  273.0 1.0 convolution_convert_fusion
  274.0 0.0 reduce-scatter.3.cloned.1.call-update
  274.0 5.6 %reduce-scatter.5.cloned.1.call-done = bf16[128,192]{0,1:T(8,128)(2,1)} async-done(((bf16[128,384]{0,1:T(8,128)(2,1)}), bf16[128,192]{0,1:T(8,128)(2,1)}) %reduce-scatter.5.cloned.1.call-update) | async-done | bytes 49168 | tf_op jit(solution)/shard_map/reduce_scatter | solution.py:105
  279.7 11.5 %reduce-scatter.3.cloned.1.call-done = bf16[128,192]{0,1:T(8,128)(2,1)} async-done(((bf16[128,384]{0,1:T(8,128)(2,1)}), bf16[128,192]{0,1:T(8,128)(2,1)}) %reduce-scatter.3.cloned.1.call-update) | async-done | bytes 49168 | tf_op jit(solution)/shard_map/reduce_scatter | solution.py:102
Async XLA Ops:
  7.2 36.2 %copy-start.6 = (bf16[48,768]{1,0:T(8,128)(2,1)S(1)}, bf16[48,768]{1,0:T(8,128)(2,1)}, u32[]{:S(2)}) copy-start(bf16[48,768]{1,0:T(8,128)(2,1)} %param.12) | copy-start | bytes 221188
  7.2 250.7 %all-reduce.3.cloned.1.call-start = ((), (), s32[]{:S(2)}) async-start(), calls=%async_computation.2 | async-start | bytes 7077888 | tf_op jit(solution)/shard_map/psum | solution.py:55
  75.7 1.1 copy-start.5
  75.7 3.4 %copy-start.7 = (bf16[48,768]{1,0:T(8,128)(2,1)S(1)}, bf16[48,768]{1,0:T(8,128)(2,1)}, u32[]{:S(2)}) copy-start(bf16[48,768]{1,0:T(8,128)(2,1)} %param.13) | copy-start | bytes 221188
  76.7 33.8 %copy-start.10 = (f32[1024]{0:T(1024)S(1)}, f32[1024]{0:T(1024)}, u32[]{:S(2)}) copy-start(f32[1024]{0:T(1024)} %param.10) | copy-start | bytes 12292
  117.7 3.3 %copy-start.8 = (bf16[128,192]{0,1:T(8,128)(2,1)S(1)}, bf16[128,192]{0,1:T(8,128)(2,1)}, u32[]{:S(2)}) copy-start(bf16[128,192]{0,1:T(8,128)(2,1)} %param.15) | copy-start | bytes 147460
  117.7 5.3 %copy-start.9 = (bf16[128,192]{0,1:T(8,128)(2,1)S(1)}, bf16[128,192]{0,1:T(8,128)(2,1)}, u32[]{:S(2)}) copy-start(bf16[128,192]{0,1:T(8,128)(2,1)} %param.14) | copy-start | bytes 147460
  117.7 162.0 %reduce-scatter.5.cloned.1.call-start = ((), (), s32[]{:S(2)}) async-start(), calls=%async_computation.4 | async-start | bytes 147456 | tf_op jit(solution)/shard_map/reduce_scatter | solution.py:105
  257.8 10.2 %copy-start = (f32[384,2304]{0,1:T(8,128)S(1)}, f32[384,2304]{0,1:T(8,128)}, u32[]{:S(2)}) copy-start(f32[384,2304]{0,1:T(8,128)} %all-reduce.3.cloned.1.call-done) | copy-start | bytes 10616836
  268.0 2.1 copy-start.3
  270.0 1.3 copy-start.1
  270.1 1.0 copy-start.4
  271.8 1.2 copy-start.2
  272.9 18.2 %reduce-scatter.3.cloned.1.call-start = ((), (), s32[]{:S(2)}) async-start(), calls=%async_computation.3 | async-start | bytes 147456 | tf_op jit(solution)/shard_map/reduce_scatter | solution.py:102
Sparse Core Ops, SparseCore 0:
  117.8 140.0 all-reduce.2
  273.1 6.5 reduce-scatter.4
  282.5 8.6 reduce-scatter.2
where the time goes:
time: 298 us
  waiting for transfers between devices  150 us (50%)
  blocking collectives  110 us (37%)
  between operations  13.9 us (5%)
  matrix products  10.6 us (4%)
  other arithmetic  9.59 us (3%)
  local copies, waits for them, and re-layouts  3.61 us (1%)
    psum x1, waiting for transfers between devices, shards(): lax.psum(jnp.concatenate([contract_rows(keys, d_gate), contract_rows(keys...  133 us
    all_gather x1, blocking collectives, shards(): lax.all_gather(gate_weight, 'tok', axis=0, tiled=True)  33.4 us
    all_gather x1, blocking collectives, shards(): lax.all_gather(down_weight, 'tok', axis=0, tiled=True)  31.4 us
    all_gather x1, blocking collectives, shards(): lax.all_gather(up_weight, 'tok', axis=0, tiled=True)  31.3 us
    reduce_scatter x1, waiting for transfers between devices, shards(): lax.psum_scatter(out_part.astype(jnp.bfloat16), 'hid', scatter_dimension=...  11.5 us
  transfers between devices with their start and end apart: 3, of which 3 were waited for; matrix products, arithmetic and copies ran while one was open for 1% of the time, Pallas kernels for 0%

commit v1 on v0

--- a/solution.py
+++ b/solution.py
@@ -1,6 +1,10 @@
+import functools
+
 import jax
 import jax.numpy as jnp
 from jax import lax
+from jax.experimental import pallas as pl
+from jax.experimental.pallas import tpu as pltpu
 from jax.sharding import PartitionSpec as P
 
 HID = 1536
@@ -31,7 +35,7 @@
     return (moved * (jnp.sqrt(wsq) / jnp.sqrt(msq + epsilon))[:, None]).astype(jnp.bfloat16)
 
 
-def shards(
+def shards_plain(
     input_keys, input_values, input_lr, gate_weight, up_weight, down_weight, queries, out_grad
 ):
     keys, values = (
@@ -109,7 +113,446 @@
     return (out_sum.astype(jnp.bfloat16), grad_sum.astype(jnp.bfloat16))
 
 
+MESH = pl.DeviceIdType.MESH
+WIDE = 2
+ANY = pl.BlockSpec(memory_space=pl.ANY)
+VM = pl.BlockSpec(memory_space=pltpu.VMEM)
+
+
+def place(tok):
+    rank = lax.axis_index("tok")
+    return lax.div(rank, WIDE), lax.rem(rank, WIDE), tok // WIDE
+
+
+def remote(src, dst, send, recv, **where):
+    return pltpu.make_async_remote_copy(
+        src_ref=src, dst_ref=dst, send_sem=send, recv_sem=recv,
+        device_id=where, device_id_type=MESH,
+    )
+
+
+def greet(always, ends=()):
+    barrier = pltpu.get_barrier_semaphore()
+
+    def tell(where):
+        pl.semaphore_signal(barrier, inc=1, device_id=where, device_id_type=MESH)
+
+    for where in always:
+        tell(where)
+    for cond, where in ends:
+        pl.when(cond)(functools.partial(tell, where))
+    if not ends:
+        pl.semaphore_wait(barrier, len(always))
+        return
+    both = ends[0][0] & ends[1][0]
+
+    @pl.when(both)
+    def _():
+        pl.semaphore_wait(barrier, len(always) + 2)
+
+    @pl.when(jnp.logical_not(both))
+    def _():
+        pl.semaphore_wait(barrier, len(always) + 1)
+
+
+UP, DOWN, SIDE, OVER = range(4)
+
+
+def spread_step(step, tok, active, own, out, send, recv, over):
+    z, x, depth = place(tok)
+
+    def pass_on(src, block, up, down):
+        def go(cond, direction, **where):
+            def start():
+                remote(src, out.at[block], send.at[direction, block], recv.at[block], **where).start()
+            if cond is None:
+                start()
+            else:
+                pl.when(cond)(start)
+        if up:
+            go(z < depth - 1, UP, tok=(z + 1) * WIDE + x)
+        if down:
+            go(z > 0, DOWN, tok=(z - 1) * WIDE + x)
+        go(None, SIDE, tok=z * WIDE + 1 - x)
+        if over is not None and not (up and down):
+            go(None, OVER, scene=over)
+
+    def arrive(block):
+        remote(out.at[block], out.at[block], send.at[0, block], recv.at[block], tok=block).wait_recv()
+
+    def body():
+        if step == 0:
+            pass_on(own, z * WIDE + x, True, True)
+            return
+
+        @pl.when(z >= step)
+        def _():
+            block = (z - step) * WIDE + x
+            arrive(block)
+            pass_on(out.at[block], block, True, False)
+
+        @pl.when(z + step < depth)
+        def _():
+            block = (z + step) * WIDE + x
+            arrive(block)
+            pass_on(out.at[block], block, False, True)
+
+    if active is None:
+        body()
+    else:
+        pl.when(active)(body)
+
+
+def spread_side(tok, active, out, send, recv, over):
+    z, x, depth = place(tok)
+
+    def take(block):
+        remote(out.at[block], out.at[block], send.at[0, block], recv.at[block], tok=block).wait_recv()
+        if over is not None:
+            remote(out.at[block], out.at[block], send.at[OVER, block], recv.at[block], scene=over).start()
+
+    def body():
+        take(z * WIDE + 1 - x)
+        for step in range(1, depth):
+            @pl.when(z >= step)
+            def _():
+                take((z - step) * WIDE + 1 - x)
+
+            @pl.when(z + step < depth)
+            def _():
+                take((z + step) * WIDE + 1 - x)
+
+    if active is None:
+        body()
+    else:
+        pl.when(active)(body)
+
+
+def spread_end(tok, active, out, send, recv, over):
+    z, x, depth = place(tok)
+
+    def sent(direction, block):
+        remote(out.at[block], out.at[block], send.at[direction, block], recv.at[block], tok=block).wait_send()
+
+    def body():
+        for level in range(depth):
+            block = level * WIDE + x
+            sent(SIDE, block)
+
+            @pl.when((z >= level) & (z < depth - 1))
+            def _():
+                sent(UP, block)
+
+            @pl.when((z <= level) & (z > 0))
+            def _():
+                sent(DOWN, block)
+            if over is not None:
+                @pl.when(z != level)
+                def _():
+                    sent(OVER, block)
+                sent(OVER, level * WIDE + 1 - x)
+
+    if active is None:
+        body()
+    else:
+        pl.when(active)(body)
+    if over is not None:
+        @pl.when(jnp.logical_not(active))
+        def _():
+            for step in range(tok):
+                @pl.when(z * WIDE + x != step)
+                def _():
+                    remote(out.at[step], out.at[step], send.at[0, step], recv.at[step], tok=step).wait_recv()
+
+
+def gather_kernel(tok, *refs):
+    rows_in, weights_in, rows_out, weights_out = refs[:4], refs[4:7], refs[7:11], refs[11:14]
+    pair_send, pair_recv, send, recv, local = refs[14:]
+    z, x, depth = place(tok)
+    scene = lax.axis_index("scene")
+    core = lax.axis_index("hid")
+    greet(
+        ({"hid": 1 - core}, {"scene": 1 - scene}, {"tok": z * WIDE + 1 - x}),
+        ((z < depth - 1, {"tok": (z + 1) * WIDE + x}), (z > 0, {"tok": (z - 1) * WIDE + x})),
+    )
+    plan = []
+    for index in range(3):
+        active = None if index == 2 else scene == index
+        over = None if index == 2 else 1 - scene
+        plan.append((active, weights_out[index], send.at[index], recv.at[index], over))
+    for index, (active, out, s, r, over) in enumerate(plan):
+        spread_step(0, tok, active, weights_in[index], out, s, r, over)
+    pairs = []
+    for index in range(4):
+        pairs.append(remote(rows_in[index], rows_out[index], pair_send.at[index], pair_recv.at[index], hid=1 - core))
+        pairs[-1].start()
+    copies = []
+    for index in range(3):
+        copies.append(pltpu.make_async_copy(weights_in[index], weights_out[index].at[z * WIDE + x], local.at[index]))
+        copies[-1].start()
+    for step in range(1, depth):
+        for index, (active, out, s, r, over) in enumerate(plan):
+            spread_step(step, tok, active, weights_in[index], out, s, r, over)
+    for active, out, s, r, over in plan:
+        spread_side(tok, active, out, s, r, over)
+    for active, out, s, r, over in plan:
+        spread_end(tok, active, out, s, r, over)
+    for copy in copies:
+        copy.wait()
+    for copy in pairs:
+        copy.wait()
+
+
+def gather(tok, rows, weights):
+    return pl.pallas_call(
+        functools.partial(gather_kernel, tok),
+        out_shape=[jax.ShapeDtypeStruct(a.shape, a.dtype) for a in rows]
+        + [jax.ShapeDtypeStruct((tok,) + a.shape, a.dtype) for a in weights],
+        in_specs=[ANY] * 7,
+        out_specs=[ANY] * 7,
+        scratch_shapes=[
+            pltpu.SemaphoreType.DMA((4,)),
+            pltpu.SemaphoreType.DMA((4,)),
+            pltpu.SemaphoreType.DMA((3, 4, tok)),
+            pltpu.SemaphoreType.DMA((3, tok)),
+            pltpu.SemaphoreType.DMA((3,)),
+        ],
+        compiler_params=pltpu.CompilerParams(collective_id=0, has_side_effects=True),
+    )(*rows, *weights)
+
+
+def join(core, mine, other, full):
+    half = mine.shape[1]
+
+    @pl.when(core == 0)
+    def _():
+        full[:, :half] = mine[...]
+        full[:, half:] = other[...]
+
+    @pl.when(core != 0)
+    def _():
+        full[:, :half] = other[...]
+        full[:, half:] = mine[...]
+
+
+def learn_kernel(chunk, keys_a, keys_b, vals_a, vals_b, lr, gate, up, down, out, keys, vals, totals):
+    core = lax.axis_index("hid")
+    join(core, keys_a, keys_b, keys)
+    join(core, vals_a, vals_b, vals)
+    totals[...] = jnp.zeros_like(totals)
+
+    def body(step, carry):
+        rows = pl.ds(pl.multiple_of(step * chunk, chunk), chunk)
+        k = keys[rows, :]
+        scaled = (lr[rows, :] * vals[rows, :].astype(jnp.float32)).astype(jnp.bfloat16)
+        key_gate = jnp.dot(k, gate[...], preferred_element_type=jnp.float32)
+        key_up = jnp.dot(k, up[...], preferred_element_type=jnp.float32)
+        back = jnp.dot(scaled, down[...], preferred_element_type=jnp.float32)
+        sigma = jax.nn.sigmoid(key_gate)
+        act = key_gate * sigma
+        key_act = (act * key_up).astype(jnp.bfloat16)
+        d_gate = (-back * key_up * (sigma * (1.0 + key_gate * (1.0 - sigma)))).astype(jnp.bfloat16)
+        d_up = (-back * act).astype(jnp.bfloat16)
+        totals[0] += contract_rows(k, d_gate)
+        totals[1] += contract_rows(k, d_up)
+        totals[2] -= contract_rows(scaled, key_act)
+        return carry
+
+    lax.fori_loop(0, keys.shape[0] // chunk, body, 0)
+    out[...] = totals[...].astype(out.dtype)
+
+
+def learn(keys_a, keys_b, vals_a, vals_b, lr, gate, up, down):
+    tokens, half = keys_a.shape
+    width = gate.shape[1]
+    return pl.pallas_call(
+        functools.partial(learn_kernel, 256),
+        out_shape=jax.ShapeDtypeStruct((3, 2 * half, width), jnp.bfloat16),
+        in_specs=[VM] * 8,
+        out_specs=VM,
+        scratch_shapes=[
+            pltpu.VMEM((tokens, 2 * half), jnp.bfloat16),
+            pltpu.VMEM((tokens, 2 * half), jnp.bfloat16),
+            pltpu.VMEM((3, 2 * half, width), jnp.float32),
+        ],
+    )(keys_a, keys_b, vals_a, vals_b, lr, gate, up, down)
+
+
+def update_kernel(tok, hidden, grads, gate, up, down, out_gate, out_up, out_down,
+                  from_side, to_z, from_z, total, stats, fresh,
+                  side_send, side_recv, z_send, z_recv, pair_send, pair_recv, send, recv, local):
+    z, x, depth = place(tok)
+    core = lax.axis_index("hid")
+    side = z * WIDE + 1 - x
+    greet(
+        ({"hid": 1 - core}, {"tok": side})
+        + tuple({"tok": lax.rem(z + step, depth) * WIDE + x} for step in range(1, depth))
+    )
+    sides = []
+    for step in range(1, depth + 1):
+        level = lax.rem(z + step, depth)
+        for index in range(3):
+            sides.append(remote(grads.at[index, level * WIDE + 1 - x], from_side.at[step - 1, index],
+                                side_send.at[step - 1, index], side_recv.at[step - 1, index], tok=side))
+            sides[-1].start()
+    alongs = []
+    for step in range(1, depth + 1):
+        level = lax.rem(z + step, depth)
+        for index in range(3):
+            sides[(step - 1) * 3 + index].wait_recv()
+            both = grads[index, level * WIDE + x].astype(jnp.float32) + from_side[step - 1, index].astype(jnp.float32)
+            if step == depth:
+                total[index] = both
+            else:
+                to_z[step - 1, index] = both.astype(jnp.bfloat16)
+                alongs.append(remote(to_z.at[step - 1, index], from_z.at[step - 1, index],
+                                     z_send.at[step - 1, index], z_recv.at[step - 1, index], tok=level * WIDE + x))
+                alongs[-1].start()
+    olds = (gate, up, down)
+    lanes = lax.broadcasted_iota(jnp.int32, stats.shape[1:], 1)
+    table = jnp.zeros(stats.shape[1:], jnp.float32)
+    for index in range(3):
+        grad = total[index]
+        for step in range(1, depth):
+            alongs[(step - 1) * 3 + index].wait_recv()
+            grad = grad + from_z[step - 1, index].astype(jnp.float32)
+        total[index] = grad
+        old = olds[index][...].astype(jnp.float32)
+        for place_in, value in enumerate((old * old, old * grad, grad * grad)):
+            table = jnp.where(lanes == 3 * index + place_in, jnp.sum(value, axis=1, keepdims=True), table)
+    stats[0] = table
+    swap = remote(stats.at[0], stats.at[1], pair_send, pair_recv, hid=1 - core)
+    swap.start()
+    swap.wait_recv()
+    table = stats[0] + stats[1]
+    outs = (out_gate, out_up, out_down)
+    plan = [(outs[i], send.at[i], recv.at[i]) for i in range(3)]
+    copies = []
+    for index in range(3):
+        wsq, cross, gsq = (
+            jnp.sum(jnp.where(lanes == 3 * index + k, table, 0.0), axis=1, keepdims=True) / hidden for k in range(3)
+        )
+        scale = step_ratio * jnp.sqrt(wsq) / jnp.sqrt(gsq + epsilon)
+        moved = olds[index][...].astype(jnp.float32) - scale * total[index]
+        msq = wsq - 2.0 * scale * cross + scale * scale * gsq
+        fresh[index] = (moved * (jnp.sqrt(wsq) / jnp.sqrt(msq + epsilon))).astype(jnp.bfloat16)
+        out, s, r = plan[index]
+        spread_step(0, tok, None, fresh.at[index], out, s, r, None)
+        copies.append(pltpu.make_async_copy(fresh.at[index], out.at[z * WIDE + x], local.at[index]))
+        copies[-1].start()
+    for step in range(1, depth):
+        for index, (out, s, r) in enumerate(plan):
+            spread_step(step, tok, None, fresh.at[index], out, s, r, None)
+    for out, s, r in plan:
+        spread_side(tok, None, out, s, r, None)
+    for out, s, r in plan:
+        spread_end(tok, None, out, s, r, None)
+    for copy in copies:
+        copy.wait()
+    for copy in sides + alongs + [swap]:
+        copy.wait_send()
+
+
+def update(tok, grads, gate, up, down):
+    rows, width = gate.shape
+    depth = tok // WIDE
+    dma = pltpu.SemaphoreType.DMA
+    blocks = (depth, 3, rows, width)
+    return pl.pallas_call(
+        functools.partial(update_kernel, tok, 2 * width),
+        out_shape=[jax.ShapeDtypeStruct((tok, rows, width), jnp.bfloat16)] * 3,
+        in_specs=[VM] * 4,
+        out_specs=[ANY] * 3,
+        scratch_shapes=[
+            pltpu.VMEM(blocks, jnp.bfloat16),
+            pltpu.VMEM(blocks, jnp.bfloat16),
+            pltpu.VMEM(blocks, jnp.bfloat16),
+            pltpu.VMEM((3, rows, width), jnp.float32),
+            pltpu.VMEM((2, rows, 128), jnp.float32),
+            pltpu.VMEM((3, rows, width), jnp.bfloat16),
+            dma((depth, 3)), dma((depth, 3)), dma((depth, 3)), dma((depth, 3)),
+            dma, dma,
+            dma((3, 4, tok)), dma((3, tok)), dma((3,)),
+        ],
+        compiler_params=pltpu.CompilerParams(collective_id=1, has_side_effects=True),
+    )(grads, gate, up, down)
+
+
+def query_kernel(q_a, q_b, g_a, g_b, gate, up, down, mine, theirs, query_rows, grad_rows, parts, got, send, recv):
+    core = lax.axis_index("hid")
+    greet(({"hid": 1 - core},))
+    join(core, q_a, q_b, query_rows)
+    join(core, g_a, g_b, grad_rows)
+    query_gate = jnp.dot(query_rows[...], gate[...], preferred_element_type=jnp.float32)
+    query_up = jnp.dot(query_rows[...], up[...], preferred_element_type=jnp.float32)
+    sigma = jax.nn.sigmoid(query_gate)
+    query_silu = query_gate * sigma
+    query_act = (query_silu * query_up).astype(jnp.bfloat16)
+    half = q_a.shape[1]
+    out_part = contract_cols(query_act, down[...])
+    parts[0, 0] = out_part[:, :half].astype(jnp.bfloat16)
+    parts[1, 0] = out_part[:, half:].astype(jnp.bfloat16)
+    first = remote(parts.at[1 - core, 0], got.at[0], send.at[0], recv.at[0], hid=1 - core)
+    first.start()
+    query_back = jnp.dot(grad_rows[...], down[...], preferred_element_type=jnp.float32)
+    q_gate_grad = (query_back * query_up * (sigma * (1.0 + query_gate * (1.0 - sigma)))).astype(jnp.bfloat16)
+    q_up_grad = (query_back * query_silu).astype(jnp.bfloat16)
+    grad_part = contract_cols(q_gate_grad, gate[...]) + contract_cols(q_up_grad, up[...])
+    parts[0, 1] = grad_part[:, :half].astype(jnp.bfloat16)
+    parts[1, 1] = grad_part[:, half:].astype(jnp.bfloat16)
+    second = remote(parts.at[1 - core, 1], got.at[1], send.at[1], recv.at[1], hid=1 - core)
+    second.start()
+    mine[...] = parts[core]
+    first.wait()
+    second.wait()
+    theirs[...] = got[...]
+
+
+def query(q_a, q_b, g_a, g_b, gate, up, down):
+    tokens, half = q_a.shape
+    pair = jax.ShapeDtypeStruct((2, tokens, half), jnp.bfloat16)
+    return pl.pallas_call(
+        query_kernel,
+        out_shape=[pair, pair],
+        in_specs=[VM] * 7,
+        out_specs=[VM] * 2,
+        scratch_shapes=[
+            pltpu.VMEM((tokens, 2 * half), jnp.bfloat16),
+            pltpu.VMEM((tokens, 2 * half), jnp.bfloat16),
+            pltpu.VMEM((2, 2, tokens, half), jnp.bfloat16),
+            pltpu.VMEM((2, tokens, half), jnp.bfloat16),
+            pltpu.SemaphoreType.DMA((2,)),
+            pltpu.SemaphoreType.DMA((2,)),
+        ],
+        compiler_params=pltpu.CompilerParams(collective_id=2, has_side_effects=True),
+    )(q_a, q_b, g_a, g_b, gate, up, down)
+
+
+def shards_fast(
+    tok, input_keys, input_values, input_lr, gate_weight, up_weight, down_weight, queries, out_grad
+):
+    rows, width = gate_weight.shape
+    keys_b, vals_b, q_b, g_b, w_gate, w_up, w_down = gather(
+        tok, (input_keys, input_values, queries, out_grad), (gate_weight, up_weight, down_weight)
+    )
+    flat = (tok * rows, width)
+    grads = learn(
+        input_keys, keys_b, input_values, vals_b, input_lr[:, None],
+        w_gate.reshape(flat), w_up.reshape(flat), w_down.reshape(flat),
+    )
+    news = update(tok, grads.reshape(3, tok, rows, width), gate_weight, up_weight, down_weight)
+    new_gate, new_up, new_down = (new.reshape(flat) for new in news)
+    mine, theirs = query(queries, q_b, out_grad, g_b, new_gate, new_up, new_down)
+    sums = [
+        (mine[i].astype(jnp.float32) + theirs[i].astype(jnp.float32)).astype(jnp.bfloat16) for i in range(2)
+    ]
+    return (sums[0], sums[1])
+
+
 def solution(mesh):
+    tok = mesh.shape["tok"]
+    fast = tok % WIDE == 0 and WIDE < tok <= 8 and mesh.shape["scene"] == 2 and mesh.shape["hid"] == 2
+    shards = functools.partial(shards_fast, tok) if fast else shards_plain
     return jax.shard_map(
         shards,
         mesh=mesh,

time: 298 us -> 101 us (0.34)
  waiting for transfers between devices: 150 us -> 0 us
  blocking collectives: 110 us -> 0 us
  Pallas kernels: 0 us -> 89.1 us
  between operations: 13.9 us -> 0.67 us
  matrix products: 10.6 us -> 0 us
  other arithmetic: 9.59 us -> 0.97 us
  local copies, waits for them, and re-layouts: 3.61 us -> 9.56 us
    psum x1 -> x0, waiting for transfers between devices: 133 us -> none  [shards(): lax.psum(jnp.concatenate([contract_rows(keys, d_gate), contract_rows(keys...]
    all_gather x7 -> x0, blocking collectives: 105 us -> none  [the longest x1 33.4 us: shards(): lax.all_gather(gate_weight, 'tok', axis=0, tiled=True)]
    pallas_call x0 -> x4, Pallas kernels: none -> 89.1 us  [the longest x1 48 us: update(): pl.pallas_call(functools.partial(update_kernel, tok, 2 * width), out_shap...]
    reduce_scatter x2 -> x0, waiting for transfers between devices: 17.1 us -> none  [the longest x1 11.5 us: shards(): lax.psum_scatter(out_part.astype(jnp.bfloat16), 'hid', scatter_dimension=...]
    dot_general x12 -> x0, matrix products: 10.6 us -> none  [the longest x3 4 us: contract_rows(): lax.dot_general(left, right, (((0,), (0,)), ((), ())), preferred_element_...]
    unnamed x22 -> x8, local copies, waits for them, and re-layouts: 0.38 us -> 8.51 us
    psum x1 -> x0, blocking collectives: 4.62 us -> none  [shards(): lax.psum((stats[0], stats[1], stats[2], stats[3], stats[4], stats[5], sta...]
    reduce_sum x1 -> x0, other arithmetic: 4.06 us -> none  [shards(): stats.append(jnp.sum(grad * grad, axis=1))]
  transfers between devices with their start and end apart: 3 -> 0, of which waited for: 3 -> 0; matrix products, arithmetic and copies ran while one was open for 1% -> 0% of each run, Pallas kernels for 0% -> 0%
where the time goes in v1:
time: 101 us; the launch traced here: 100 us
  Pallas kernels  89.1 us (88%)
  local copies, waits for them, and re-layouts  9.56 us (9%)
    pallas_call x1, Pallas kernels, update(): pl.pallas_call(functools.partial(update_kernel, tok, 2 * width), out_shap...  48 us
    pallas_call x1, Pallas kernels, gather(): pl.pallas_call(functools.partial(gather_kernel, tok), out_shape=[jax.Shap...  25.7 us
    pallas_call x1, Pallas kernels, learn(): pl.pallas_call(functools.partial(learn_kernel, 256), out_shape=jax.ShapeD...  10.2 us
    unnamed x8, local copies, waits for them, and re-layouts  8.51 us
    pallas_call x1, Pallas kernels, query(): pl.pallas_call(query_kernel, out_shape=[pair, pair], in_specs=[VM] * 7, o...  5.15 us

profile of v1, /device:TPU:0, one launch (start us, length us, event | category | flops | bytes accessed | tf_op | source)
XLA Modules:
  0.0 100.2 jit_solution(6790064890045943277)
XLA Ops:
  0.6 0.0 copy-start
  0.6 1.5 %copy.27.refs_2_.q_a = bf16[128,192]{1,0:T(8,128)(2,1)} copy(bf16[128,192]{0,1:T(8,128)(2,1)} %param.14) | data formatting | bytes 98304 | tf_op args[6]
  2.2 1.5 %copy.23.refs_3_.g_a = bf16[128,192]{1,0:T(8,128)(2,1)} copy(bf16[128,192]{0,1:T(8,128)(2,1)} %param.15) | data formatting | bytes 98304 | tf_op args[7]
  3.7 2.0 %copy.20.refs_0_.keys_a = bf16[1024,192]{1,0:T(8,128)(2,1)} copy(bf16[1024,192]{0,1:T(8,128)(2,1)} %param.8) | data formatting | bytes 786432 | tf_op args[0]
  5.7 2.0 %copy.21.refs_1_.vals_a = bf16[1024,192]{1,0:T(8,128)(2,1)} copy(bf16[1024,192]{0,1:T(8,128)(2,1)} %param.9) | data formatting | bytes 786432 | tf_op args[1]
  7.7 0.0 copy-done
  7.7 1.1 %copy.26.lr = f32[1024,1]{1,0:T(8,128)} copy(f32[1024,1]{0,1:T(1,128)S(1)} %bitcast.19) | data formatting | bytes 8192 | tf_op jit(solution)/shard_map/broadcast_in_dim | solution.py:540
  8.8 25.7 %shard_map.95 = (bf16[1024,192]{1,0:T(8,128)(2,1)}, bf16[1024,192]{1,0:T(8,128)(2,1)}, bf16[128,192]{1,0:T(8,128)(2,1)}, bf16[128,192]{1,0:T(8,128)(2,1)}, bf16[...) custom-call(bf16[1024,192]{1,0:T(8,128)(2,1)} %copy.20.refs_0_.keys_a, ...), custom_call_target="tpu_custom_call" | custom-call | tf_op jit(solution)/shard_map/pallas_call | solution.py:307
  34.4 10.2 %shard_map.96 = bf16[3,384,768]{2,1,0:T(8,128)(2,1)} custom-call(bf16[1024,192]{1,0:T(8,128)(2,1)} %copy.20.refs_0_.keys_a, bf16[1024,192]{1,0:T(8,128)(2,1)} %get-tuple-element.16.keys_b, bf16[1024,192]{1,0:T(8,128)(2,1)} %copy.21.refs_1_.vals_a, bf16[1024,192]{1,0:T(8,128)(2,1)} %get-tuple-element.17.vals_b, f32[1024,1]{1,0:T(8,128)} %copy.26.lr, ...), custom_call_target="tpu_custom_call" | custom-call | tf_op jit(solution)/shard_map/pallas_call | solution.py:368
  44.7 48.0 %shard_map.97 = (bf16[8,48,768]{2,1,0:T(8,128)(2,1)}, bf16[8,48,768]{2,1,0:T(8,128)(2,1)}, bf16[8,48,768]{2,1,0:T(8,128)(2,1)}) custom-call(bf16[3,8,48,768]{3,2,1,0:T(8,128)(2,1)} %bitcast.12, bf16[48,768]{1,0:T(8,128)(2,1)} %gate.1, bf16[48,768]{1,0:T(8,128)(2,1)} %up.1, bf16[48,768]{1,0:T(8,128)(2,1)} %down.1), custom_call_target="tpu_custom_call" | custom-call | tf_op jit(solution)/shard_map/pallas_call | solution.py:461
  92.7 5.2 %shard_map.98 = (bf16[2,128,192]{2,1,0:T(8,128)(2,1)}, bf16[2,128,192]{2,1,0:T(8,128)(2,1)}) custom-call(bf16[128,192]{1,0:T(8,128)(2,1)} %copy.27.refs_2_.q_a, bf16[128,192]{1,0:T(8,128)(2,1)} %get-tuple-element.14.q_b, bf16[128,192]{1,0:T(8,128)(2,1)} %copy.23.refs_3_.g_a, bf16[128,192]{1,0:T(8,128)(2,1)} %get-tuple-element.15.g_b, ...), custom_call_target="tpu_custom_call" | custom-call | tf_op jit(solution)/shard_map/pallas_call | solution.py:514
  97.8 1.0 fusion.1
  98.8 0.7 copy.30
  99.5 0.7 copy.29
Async XLA Ops:
  0.6 7.1 %copy-start = (f32[1024]{0:T(1024)S(1)}, f32[1024]{0:T(1024)}, u32[]{:S(2)}) copy-start(f32[1024]{0:T(1024)} %param.10) | copy-start | bytes 12292

commit v2 on v0

--- a/solution.py
+++ b/solution.py
@@ -1,6 +1,10 @@
+import functools
+
 import jax
 import jax.numpy as jnp
 from jax import lax
+from jax.experimental import pallas as pl
+from jax.experimental.pallas import tpu as pltpu
 from jax.sharding import PartitionSpec as P
 
 HID = 1536
@@ -31,7 +35,7 @@
     return (moved * (jnp.sqrt(wsq) / jnp.sqrt(msq + epsilon))[:, None]).astype(jnp.bfloat16)
 
 
-def shards(
+def shards_plain(
     input_keys, input_values, input_lr, gate_weight, up_weight, down_weight, queries, out_grad
 ):
     keys, values = (
@@ -109,7 +113,407 @@
     return (out_sum.astype(jnp.bfloat16), grad_sum.astype(jnp.bfloat16))
 
 
+MESH = pl.DeviceIdType.MESH
+WIDE = 2
+ANY = pl.BlockSpec(memory_space=pl.ANY)
+VM = pl.BlockSpec(memory_space=pltpu.VMEM)
+
+
+def place(tok):
+    rank = lax.axis_index("tok")
+    return lax.div(rank, WIDE), lax.rem(rank, WIDE), tok // WIDE
+
+
+def remote(src, dst, send, recv, **where):
+    return pltpu.make_async_remote_copy(
+        src_ref=src, dst_ref=dst, send_sem=send, recv_sem=recv,
+        device_id=where, device_id_type=MESH,
+    )
+
+
+def greet(peers):
+    barrier = pltpu.get_barrier_semaphore()
+    for where in peers:
+        pl.semaphore_signal(barrier, inc=1, device_id=where, device_id_type=MESH)
+    pl.semaphore_wait(barrier, len(peers))
+
+
+UP, DOWN, SIDE, OVER = range(4)
+
+
+def spread_step(step, tok, active, own, out, send, recv, over):
+    z, x, depth = place(tok)
+
+    def pass_on(src, block, up, down):
+        def go(cond, direction, **where):
+            def start():
+                remote(src, out.at[block], send.at[direction, block], recv.at[block], **where).start()
+            if cond is None:
+                start()
+            else:
+                pl.when(cond)(start)
+        if up:
+            go(z < depth - 1, UP, tok=(z + 1) * WIDE + x)
+        if down:
+            go(z > 0, DOWN, tok=(z - 1) * WIDE + x)
+        go(None, SIDE, tok=z * WIDE + 1 - x)
+        if over is not None and not (up and down):
+            go(None, OVER, scene=over)
+
+    def arrive(block):
+        remote(out.at[block], out.at[block], send.at[0, block], recv.at[block], tok=block).wait_recv()
+
+    def body():
+        if step == 0:
+            pass_on(own, z * WIDE + x, True, True)
+            return
+
+        @pl.when(z >= step)
+        def _():
+            block = (z - step) * WIDE + x
+            arrive(block)
+            pass_on(out.at[block], block, True, False)
+
+        @pl.when(z + step < depth)
+        def _():
+            block = (z + step) * WIDE + x
+            arrive(block)
+            pass_on(out.at[block], block, False, True)
+
+    if active is None:
+        body()
+    else:
+        pl.when(active)(body)
+
+
+def spread_side(tok, active, out, send, recv, over=None):
+    z, x, depth = place(tok)
+
+    def take(block):
+        remote(out.at[block], out.at[block], send.at[0, block], recv.at[block], tok=block).wait_recv()
+        if over is not None:
+            remote(out.at[block], out.at[block], send.at[OVER, block], recv.at[block], scene=over).start()
+
+    def body():
+        take(z * WIDE + 1 - x)
+        for step in range(1, depth):
+            @pl.when(z >= step)
+            def _():
+                take((z - step) * WIDE + 1 - x)
+
+            @pl.when(z + step < depth)
+            def _():
+                take((z + step) * WIDE + 1 - x)
+
+    if active is None:
+        body()
+    else:
+        pl.when(active)(body)
+
+
+def spread_end(tok, active, out, send, recv, over):
+    z, x, depth = place(tok)
+
+    def sent(direction, block):
+        remote(out.at[block], out.at[block], send.at[direction, block], recv.at[block], tok=block).wait_send()
+
+    def body():
+        for level in range(depth):
+            block = level * WIDE + x
+            sent(SIDE, block)
+
+            @pl.when((z >= level) & (z < depth - 1))
+            def _():
+                sent(UP, block)
+
+            @pl.when((z <= level) & (z > 0))
+            def _():
+                sent(DOWN, block)
+            if over is not None:
+                @pl.when(z != level)
+                def _():
+                    sent(OVER, block)
+                sent(OVER, level * WIDE + 1 - x)
+
+    if active is None:
+        body()
+    else:
+        pl.when(active)(body)
+
+
+def spread_over(tok, active, out, send, recv):
+    z, x, depth = place(tok)
+
+    @pl.when(jnp.logical_not(active))
+    def _():
+        for block in range(tok):
+            @pl.when(z * WIDE + x != block)
+            def _():
+                remote(out.at[block], out.at[block], send.at[0, block], recv.at[block], tok=block).wait_recv()
+
+
+def whole_kernel(
+    tok, hidden, chunk,
+    keys_in, vals_in, lr, q_in, g_in, gate_in, up_in, down_in,
+    mine, theirs,
+    keys, vals, q, g, olds, scaled, key_gate, key_up, key_act, d_gate, d_up,
+    total, grads, from_side, to_z, from_z, stats, fresh, news, parts, got,
+    pair_send, pair_recv, pair_local, old_send, old_recv, old_local,
+    side_send, side_recv, z_send, z_recv, stat_send, stat_recv,
+    new_send, new_recv, new_local, part_send, part_recv,
+):
+    z, x, depth = place(tok)
+    scene = lax.axis_index("scene")
+    core = lax.axis_index("hid")
+    me = z * WIDE + x
+    side = z * WIDE + 1 - x
+    f32, bf16 = jnp.float32, jnp.bfloat16
+    rows, width = gate_in.shape
+    wide = tok * rows
+    levels = [lax.rem(z + step, depth) for step in range(1, depth + 1)]
+    greet(
+        ({"hid": 1 - core}, {"scene": 1 - scene}, {"tok": side})
+        + tuple({"tok": level * WIDE + x} for level in levels[:-1])
+    )
+
+    waits = []
+    plan = []
+    for index in range(3):
+        active = None if index == 2 else scene == index
+        over = None if index == 2 else 1 - scene
+        plan.append((active, olds.at[index], old_send.at[index], old_recv.at[index], over))
+    for index, own in enumerate((gate_in, up_in, down_in)):
+        active, out, s, r, over = plan[index]
+        spread_step(0, tok, active, own, out, s, r, over)
+    copies = []
+    pairs = []
+    for index, (own, full) in enumerate(((keys_in, keys), (vals_in, vals), (q_in, q), (g_in, g))):
+        pairs.append(remote(own, full.at[core], pair_send.at[index], pair_recv.at[index], hid=1 - core))
+        pairs[-1].start()
+        copies.append(pltpu.make_async_copy(own, full.at[core], pair_local.at[index]))
+        copies[-1].start()
+    for index, own in enumerate((gate_in, up_in, down_in)):
+        copies.append(pltpu.make_async_copy(own, olds.at[index, me], old_local.at[index]))
+        copies[-1].start()
+    for step in range(1, depth):
+        for active, out, s, r, over in plan:
+            spread_step(step, tok, active, None, out, s, r, over)
+    for active, out, s, r, over in plan[:2]:
+        spread_side(tok, active, out, s, r, over)
+    for active, out, s, r, over in plan[:2]:
+        spread_over(tok, active, out, s, r)
+    for copy in copies:
+        copy.wait()
+    for copy in pairs:
+        copy.wait_recv()
+
+    def forward(step, carry):
+        at = pl.ds(pl.multiple_of(step * chunk, chunk), chunk)
+        k = keys[:, :, at].reshape(wide, chunk)
+        a = contract_rows(k, olds[0].reshape(wide, width))
+        b = contract_rows(k, olds[1].reshape(wide, width))
+        key_gate[at, :] = a
+        key_up[at, :] = b
+        key_act[at, :] = (a * jax.nn.sigmoid(a) * b).astype(bf16)
+        v = vals[:, :, at].reshape(wide, chunk).astype(f32)
+        scaled[:, at] = (lr[:, at] * v).astype(bf16)
+        return carry
+
+    def backward(step, carry):
+        at = pl.ds(pl.multiple_of(step * chunk, chunk), chunk)
+        back = contract_rows(scaled[:, at], olds[2].reshape(wide, width))
+        a = key_gate[at, :]
+        sigma = jax.nn.sigmoid(a)
+        d_gate[at, :] = (-back * key_up[at, :] * (sigma * (1.0 + a * (1.0 - sigma)))).astype(bf16)
+        d_up[at, :] = (-back * (a * sigma)).astype(bf16)
+        return carry
+
+    sides = {}
+    alongs = {}
+    swaps = {}
+
+    def emit(index, grad):
+        grad = grad.reshape(tok, rows, width)
+        total[index] = grad
+        grads[index] = grad.astype(bf16)
+        for step, level in enumerate(levels):
+            copy = remote(grads.at[index, level * WIDE + 1 - x], from_side.at[index, step],
+                          side_send.at[index, step], side_recv.at[index, step], tok=side)
+            copy.start()
+            sides[index, step] = copy
+
+    def relay(index):
+        for step, level in enumerate(levels):
+            sides[index, step].wait_recv()
+            both = total[index, level * WIDE + x] + from_side[index, step].astype(f32)
+            if step == depth - 1:
+                total[index, me] = both
+            else:
+                to_z[index, step] = both.astype(bf16)
+                copy = remote(to_z.at[index, step], from_z.at[index, step],
+                              z_send.at[index, step], z_recv.at[index, step], tok=level * WIDE + x)
+                copy.start()
+                alongs[index, step] = copy
+
+    lanes = lax.broadcasted_iota(jnp.int32, (rows, 128), 1)
+
+    def measure(index):
+        grad = total[index, me]
+        for step in range(depth - 1):
+            alongs[index, step].wait_recv()
+            grad = grad + from_z[index, step].astype(f32)
+        total[index, me] = grad
+        old = olds[index, me].astype(f32)
+        table = jnp.zeros((rows, 128), f32)
+        for lane, value in enumerate((old * old, old * grad, grad * grad)):
+            table = jnp.where(lanes == lane, jnp.sum(value, axis=1, keepdims=True), table)
+        stats[index, 0] = table
+        copy = remote(stats.at[index, 0], stats.at[index, 1], stat_send.at[index], stat_recv.at[index], hid=1 - core)
+        copy.start()
+        swaps[index] = copy
+
+    renewed = [(None, news.at[i], new_send.at[i], new_recv.at[i], None) for i in range(3)]
+    places = []
+
+    def apply(index):
+        swaps[index].wait_recv()
+        table = (stats[index, 0] + stats[index, 1]) / hidden
+        wsq, cross, gsq = (
+            jnp.sum(jnp.where(lanes == lane, table, 0.0), axis=1, keepdims=True) for lane in range(3)
+        )
+        scale = step_ratio * jnp.sqrt(wsq) / jnp.sqrt(gsq + epsilon)
+        moved = olds[index, me].astype(f32) - scale * total[index, me]
+        msq = wsq - 2.0 * scale * cross + scale * scale * gsq
+        fresh[index] = (moved * (jnp.sqrt(wsq) / jnp.sqrt(msq + epsilon))).astype(bf16)
+        active, out, s, r, over = renewed[index]
+        spread_step(0, tok, active, fresh.at[index], out, s, r, over)
+        places.append(pltpu.make_async_copy(fresh.at[index], out.at[me], new_local.at[index]))
+        places[-1].start()
+
+    def pass_new(step, index):
+        active, out, s, r, over = renewed[index]
+        spread_step(step, tok, active, None, out, s, r, over)
+
+    steps = keys.shape[2] // chunk
+    lax.fori_loop(0, steps, forward, 0)
+    emit(2, -jnp.dot(scaled[...], key_act[...], preferred_element_type=f32))
+    spread_side(tok, *plan[2])
+    lax.fori_loop(0, steps, backward, 0)
+    all_keys = keys[...].reshape(wide, keys.shape[2])
+    emit(0, jnp.dot(all_keys, d_gate[...], preferred_element_type=f32))
+    relay(2)
+    emit(1, jnp.dot(all_keys, d_up[...], preferred_element_type=f32))
+    relay(0)
+    measure(2)
+    relay(1)
+    apply(2)
+    measure(0)
+    apply(0)
+    measure(1)
+    apply(1)
+    for step in range(1, depth):
+        for index in (2, 0, 1):
+            pass_new(step, index)
+
+    def fetch(index):
+        spread_side(tok, *renewed[index])
+        places[(2, 0, 1).index(index)].wait()
+        return news[index].reshape(wide, width)
+
+    half, count = q.shape[1:]
+    all_q = q[...].reshape(wide, count)
+    all_g = g[...].reshape(wide, count)
+    down = fetch(2)
+    query_back = contract_rows(all_g, down)
+    gate = fetch(0)
+    query_gate = contract_rows(all_q, gate)
+    sigma = jax.nn.sigmoid(query_gate)
+    query_silu = query_gate * sigma
+    q_up_grad = (query_back * query_silu).astype(bf16)
+    up = fetch(1)
+    query_up = contract_rows(all_q, up)
+
+    def hand(index, part):
+        parts[:, index] = part.reshape(2, half, count).astype(bf16)
+        copy = remote(parts.at[1 - core, index], got.at[index], part_send.at[index], part_recv.at[index], hid=1 - core)
+        copy.start()
+        return copy
+
+    first = hand(0, contract_cols(down, (query_silu * query_up).astype(bf16)))
+    q_gate_grad = (query_back * query_up * (sigma * (1.0 + query_gate * (1.0 - sigma)))).astype(bf16)
+    second = hand(1, contract_cols(gate, q_gate_grad) + contract_cols(up, q_up_grad))
+    mine[...] = parts[core]
+    for entry in plan + renewed:
+        spread_end(tok, *entry)
+    for copy in pairs + list(sides.values()) + list(alongs.values()) + list(swaps.values()):
+        copy.wait_send()
+    first.wait()
+    second.wait()
+    theirs[...] = got[...]
+
+
+def shards_fast(
+    tok, input_keys, input_values, input_lr, gate_weight, up_weight, down_weight, queries, out_grad
+):
+    rows, width = gate_weight.shape
+    tokens, half = input_keys.shape
+    count = queries.shape[0]
+    depth = tok // WIDE
+    f32, bf16, dma = jnp.float32, jnp.bfloat16, pltpu.SemaphoreType.DMA
+    pair = jax.ShapeDtypeStruct((2, half, count), bf16)
+    blocks = (3, tok, rows, width)
+    along = (3, depth, rows, width)
+    mine, theirs = pl.pallas_call(
+        functools.partial(whole_kernel, tok, 2 * width, 256),
+        out_shape=[pair, pair],
+        in_specs=[ANY, ANY, VM, ANY, ANY, ANY, ANY, ANY],
+        out_specs=[VM, VM],
+        scratch_shapes=[
+            pltpu.VMEM((2, half, tokens), bf16),
+            pltpu.VMEM((2, half, tokens), bf16),
+            pltpu.VMEM((2, half, count), bf16),
+            pltpu.VMEM((2, half, count), bf16),
+            pltpu.VMEM(blocks, bf16),
+            pltpu.VMEM((2 * half, tokens), bf16),
+            pltpu.VMEM((tokens, width), f32),
+            pltpu.VMEM((tokens, width), f32),
+            pltpu.VMEM((tokens, width), bf16),
+            pltpu.VMEM((tokens, width), bf16),
+            pltpu.VMEM((tokens, width), bf16),
+            pltpu.VMEM(blocks, f32),
+            pltpu.VMEM(blocks, bf16),
+            pltpu.VMEM(along, bf16),
+            pltpu.VMEM(along, bf16),
+            pltpu.VMEM(along, bf16),
+            pltpu.VMEM((3, 2, rows, 128), f32),
+            pltpu.VMEM((3, rows, width), bf16),
+            pltpu.VMEM(blocks, bf16),
+            pltpu.VMEM((2, 2, half, count), bf16),
+            pltpu.VMEM((2, half, count), bf16),
+            dma((4,)), dma((4,)), dma((4,)),
+            dma((3, 4, tok)), dma((3, tok)), dma((3,)),
+            dma((3, depth)), dma((3, depth)), dma((3, depth)), dma((3, depth)),
+            dma((3,)), dma((3,)),
+            dma((3, 4, tok)), dma((3, tok)), dma((3,)),
+            dma((2,)), dma((2,)),
+        ],
+        compiler_params=pltpu.CompilerParams(
+            collective_id=0, has_side_effects=True, vmem_limit_bytes=50 * 1024 * 1024
+        ),
+    )(
+        input_keys.T, input_values.T, input_lr.reshape(1, tokens), queries.T, out_grad.T,
+        gate_weight, up_weight, down_weight,
+    )
+    sums = [
+        (mine[i].astype(f32) + theirs[i].astype(f32)).astype(bf16).T for i in range(2)
+    ]
+    return (sums[0], sums[1])
+
+
 def solution(mesh):
+    tok = mesh.shape["tok"]
+    fast = tok % WIDE == 0 and WIDE < tok <= 8 and mesh.shape["scene"] == 2 and mesh.shape["hid"] == 2
+    shards = functools.partial(shards_fast, tok) if fast else shards_plain
     return jax.shard_map(
         shards,
         mesh=mesh,

time: 298 us -> 81.1 us (0.27)
  waiting for transfers between devices: 150 us -> 0 us
  blocking collectives: 110 us -> 0 us
  Pallas kernels: 0 us -> 72.4 us
  between operations: 13.9 us -> 0.66 us
  matrix products: 10.6 us -> 0 us
  other arithmetic: 9.59 us -> 0.66 us
  local copies, waits for them, and re-layouts: 3.61 us -> 6.92 us
    psum x1 -> x0, waiting for transfers between devices: 133 us -> none  [shards(): lax.psum(jnp.concatenate([contract_rows(keys, d_gate), contract_rows(keys...]
    all_gather x7 -> x0, blocking collectives: 105 us -> none  [the longest x1 33.4 us: shards(): lax.all_gather(gate_weight, 'tok', axis=0, tiled=True)]
    pallas_call x0 -> x1, Pallas kernels: none -> 72.4 us  [shards_fast(): pl.pallas_call(functools.partial(whole_kernel, tok, 2 * width, 256), out_...]
    reduce_scatter x2 -> x0, waiting for transfers between devices: 17.1 us -> none  [the longest x1 11.5 us: shards(): lax.psum_scatter(out_part.astype(jnp.bfloat16), 'hid', scatter_dimension=...]
    dot_general x12 -> x0, matrix products: 10.6 us -> none  [the longest x3 4 us: contract_rows(): lax.dot_general(left, right, (((0,), (0,)), ((), ())), preferred_element_...]
    unnamed x22 -> x16, local copies, waits for them, and re-layouts: 0.38 us -> 6.92 us
    psum x1 -> x0, blocking collectives: 4.62 us -> none  [shards(): lax.psum((stats[0], stats[1], stats[2], stats[3], stats[4], stats[5], sta...]
    reduce_sum x1 -> x0, other arithmetic: 4.06 us -> none  [shards(): stats.append(jnp.sum(grad * grad, axis=1))]
  transfers between devices with their start and end apart: 3 -> 0, of which waited for: 3 -> 0; matrix products, arithmetic and copies ran while one was open for 1% -> 0% of each run, Pallas kernels for 0% -> 0%
where the time goes in v2:
time: 81.1 us; the launch traced here: 80.6 us
  Pallas kernels  72.4 us (89%)
  local copies, waits for them, and re-layouts  6.92 us (9%)
    pallas_call x1, Pallas kernels, shards_fast(): pl.pallas_call(functools.partial(whole_kernel, tok, 2 * width, 256), out_...  72.4 us
    unnamed x16, local copies, waits for them, and re-layouts  6.92 us

profile of v2, /device:TPU:0, one launch (start us, length us, event | category | flops | bytes accessed | tf_op | source)
XLA Modules:
  0.0 80.6 jit_solution(12024466127710523439)
XLA Ops:
  0.6 0.0 copy-start.7
  0.6 0.7 copy-done.7
  1.3 0.0 copy-start
  1.3 1.0 %copy-done = bf16[1024,192]{0,1:T(8,128)(2,1)S(1)} copy-done((bf16[1024,192]{0,1:T(8,128)(2,1)S(1)}, bf16[1024,192]{0,1:T(8,128)(2,1)}, u32[]{:S(2)}) %copy-start) | copy-done | bytes 393240
  2.3 0.0 copy-start.1
  2.3 1.0 %copy-done.1 = bf16[1024,192]{0,1:T(8,128)(2,1)S(1)} copy-done((bf16[1024,192]{0,1:T(8,128)(2,1)S(1)}, bf16[1024,192]{0,1:T(8,128)(2,1)}, u32[]{:S(2)}) %copy-start.1) | copy-done | bytes 393240
  3.3 0.0 copy-start.2
  3.3 0.9 %copy-done.2 = bf16[48,768]{1,0:T(8,128)(2,1)S(1)} copy-done((bf16[48,768]{1,0:T(8,128)(2,1)S(1)}, bf16[48,768]{1,0:T(8,128)(2,1)}, u32[]{:S(2)}) %copy-start.2) | copy-done | bytes 73752
  4.2 0.0 copy-start.3
  4.2 0.9 %copy-done.3 = bf16[48,768]{1,0:T(8,128)(2,1)S(1)} copy-done((bf16[48,768]{1,0:T(8,128)(2,1)S(1)}, bf16[48,768]{1,0:T(8,128)(2,1)}, u32[]{:S(2)}) %copy-start.3) | copy-done | bytes 73752
  5.1 0.0 copy-start.4
  5.1 0.9 %copy-done.4 = bf16[48,768]{1,0:T(8,128)(2,1)S(1)} copy-done((bf16[48,768]{1,0:T(8,128)(2,1)S(1)}, bf16[48,768]{1,0:T(8,128)(2,1)}, u32[]{:S(2)}) %copy-start.4) | copy-done | bytes 73752
  6.0 0.0 copy-start.5
  6.0 0.8 copy-done.5
  6.8 0.0 copy-start.6
  6.8 0.8 copy-done.6
  7.6 72.4 %shard_map.95 = (bf16[2,192,128]{2,1,0:T(8,128)(2,1)S(1)}, bf16[2,192,128]{2,1,0:T(8,128)(2,1)S(1)}) custom-call(bf16[192,1024]{1,0:T(8,128)(2,1)S(1)} %bitcast.13, bf16[192,1024]{1,0:T(8,128)(2,1)S(1)} %bitcast.14, f32[1,1024]{1,0:T(1,128)S(1)} %bitcast.17, bf16[192,128]{1,0:T(8,128)(2,1)S(1)} %bitcast.15, bf16[192,128]{1,0:T(8,128)(2,1)S(1)} %bitcast.16, ...), custom_call_target="tpu_custom_call" | custom-call | tf_op jit(solution)/shard_map/pallas_call | solution.py:466
  80.0 0.7 fusion.1
Async XLA Ops:
  0.6 0.7 copy-start.7
  1.3 1.0 %copy-start = (bf16[1024,192]{0,1:T(8,128)(2,1)S(1)}, bf16[1024,192]{0,1:T(8,128)(2,1)}, u32[]{:S(2)}) copy-start(bf16[1024,192]{0,1:T(8,128)(2,1)} %param.8) | copy-start | bytes 1179652
  2.3 1.0 %copy-start.1 = (bf16[1024,192]{0,1:T(8,128)(2,1)S(1)}, bf16[1024,192]{0,1:T(8,128)(2,1)}, u32[]{:S(2)}) copy-start(bf16[1024,192]{0,1:T(8,128)(2,1)} %param.9) | copy-start | bytes 1179652
  3.3 0.9 %copy-start.2 = (bf16[48,768]{1,0:T(8,128)(2,1)S(1)}, bf16[48,768]{1,0:T(8,128)(2,1)}, u32[]{:S(2)}) copy-start(bf16[48,768]{1,0:T(8,128)(2,1)} %gate_in.1) | copy-start | bytes 221188
  4.2 0.9 %copy-start.3 = (bf16[48,768]{1,0:T(8,128)(2,1)S(1)}, bf16[48,768]{1,0:T(8,128)(2,1)}, u32[]{:S(2)}) copy-start(bf16[48,768]{1,0:T(8,128)(2,1)} %up_in.1) | copy-start | bytes 221188
  5.1 0.9 %copy-start.4 = (bf16[48,768]{1,0:T(8,128)(2,1)S(1)}, bf16[48,768]{1,0:T(8,128)(2,1)}, u32[]{:S(2)}) copy-start(bf16[48,768]{1,0:T(8,128)(2,1)} %down_in.1) | copy-start | bytes 221188
  6.0 0.8 copy-start.5
  6.8 0.8 copy-start.6

commit v3 on v2

--- a/solution.py
+++ b/solution.py
@@ -115,7 +115,7 @@
 
 MESH = pl.DeviceIdType.MESH
 WIDE = 2
-ANY = pl.BlockSpec(memory_space=pl.ANY)
+HBM = pl.BlockSpec(memory_space=pltpu.HBM)
 VM = pl.BlockSpec(memory_space=pltpu.VMEM)
 
 
@@ -466,7 +466,7 @@
     mine, theirs = pl.pallas_call(
         functools.partial(whole_kernel, tok, 2 * width, 256),
         out_shape=[pair, pair],
-        in_specs=[ANY, ANY, VM, ANY, ANY, ANY, ANY, ANY],
+        in_specs=[HBM, HBM, VM, HBM, HBM, HBM, HBM, HBM],
         out_specs=[VM, VM],
         scratch_shapes=[
             pltpu.VMEM((2, half, tokens), bf16),
@@ -498,7 +498,7 @@
             dma((2,)), dma((2,)),
         ],
         compiler_params=pltpu.CompilerParams(
-            collective_id=0, has_side_effects=True, vmem_limit_bytes=50 * 1024 * 1024
+            collective_id=0, has_side_effects=True, vmem_limit_bytes=67_000_000
         ),
     )(
         input_keys.T, input_values.T, input_lr.reshape(1, tokens), queries.T, out_grad.T,

time: 81.1 us -> 76.4 us (0.942)
  local copies, waits for them, and re-layouts: 6.92 us -> 0 us
  Pallas kernels: 72.4 us -> 74.1 us
  other arithmetic: 0.66 us -> 1.54 us
    unnamed x16 -> x0, local copies, waits for them, and re-layouts: 6.92 us -> none
    pallas_call x1, Pallas kernels: 72.4 us -> 74.1 us  [shards_fast(): pl.pallas_call(functools.partial(whole_kernel, tok, 2 * width, 256), out_...]
    transpose x1, other arithmetic: 0.66 us -> 1.54 us  [shards_fast(): (mine[i].astype(f32) + theirs[i].astype(f32)).astype(bf16)]
where the time goes in v3:
time: 76.4 us; the launch traced here: 76.2 us
  Pallas kernels  74.1 us (97%)
  other arithmetic  1.54 us (2%)
    pallas_call x1, Pallas kernels, shards_fast(): pl.pallas_call(functools.partial(whole_kernel, tok, 2 * width, 256), out_...  74.1 us
    transpose x1, other arithmetic, shards_fast(): (mine[i].astype(f32) + theirs[i].astype(f32)).astype(bf16)  1.54 us

profile of v3, /device:TPU:0, one launch (start us, length us, event | category | flops | bytes accessed | tf_op | source)
XLA Modules:
  0.0 76.2 jit_solution(11126430294591955987)
XLA Ops:
  0.6 74.1 %shard_map.95 = (bf16[2,192,128]{2,1,0:T(8,128)(2,1)}, bf16[2,192,128]{2,1,0:T(8,128)(2,1)}) custom-call(bf16[192,1024]{1,0:T(8,128)(2,1)} %bitcast.13, bf16[192,1024]{1,0:T(8,128)(2,1)} %bitcast.14, f32[1,1024]{1,0:T(1,128)} %bitcast.17, bf16[192,128]{1,0:T(8,128)(2,1)} %bitcast.15, bf16[192,128]{1,0:T(8,128)(2,1)} %bitcast.16, bf16[48,768]{1,0:T(8,128)(2,1)} %gate_in.1, ...), custom_call_target="tpu_custom_call" | custom-call | tf_op jit(solution)/shard_map/pallas_call | solution.py:466
  74.7 1.5 %fusion.1 = (bf16[128,192]{0,1:T(8,128)(2,1)}, bf16[128,192]{0,1:T(8,128)(2,1)}) fusion(bf16[2,192,128]{2,1,0:T(8,128)(2,1)} %get-tuple-element.5, bf16[2,192,128]{2,1,0:T(8,128)(2,1)} %get-tuple-element.4), kind=kLoop, calls=%fused_computation.3 | loop fusion | flops 196608 | bytes 294912 | tf_op jit(solution)/shard_map/transpose | solution.py:508

commit v4 on v3

--- a/solution.py
+++ b/solution.py
@@ -409,10 +409,11 @@
     apply(2)
     measure(0)
     apply(0)
+    pass_new(1, 2)
     measure(1)
     apply(1)
-    for step in range(1, depth):
-        for index in (2, 0, 1):
+    for index in (2, 0, 1):
+        for step in range(2 if index == 2 else 1, depth):
             pass_new(step, index)
 
     def fetch(index):

time: 76.4 us -> 79.4 us (1.039)
  Pallas kernels: 74.1 us -> 77 us
    pallas_call x1, Pallas kernels: 74.1 us -> 77 us  [shards_fast(): pl.pallas_call(functools.partial(whole_kernel, tok, 2 * width, 256), out_...]
where the time goes in v4:
time: 79.4 us; the launch traced here: 79.1 us
  Pallas kernels  77 us (97%)
  other arithmetic  1.54 us (2%)
    pallas_call x1, Pallas kernels, shards_fast(): pl.pallas_call(functools.partial(whole_kernel, tok, 2 * width, 256), out_...  77 us

profile of v4, /device:TPU:0, one launch (start us, length us, event | category | flops | bytes accessed | tf_op | source)
XLA Modules:
  0.0 79.1 jit_solution(16771745064680554211)
XLA Ops:
  0.6 77.0 %shard_map.95 = (bf16[2,192,128]{2,1,0:T(8,128)(2,1)}, bf16[2,192,128]{2,1,0:T(8,128)(2,1)}) custom-call(bf16[192,1024]{1,0:T(8,128)(2,1)} %bitcast.13, bf16[192,1024]{1,0:T(8,128)(2,1)} %bitcast.14, f32[1,1024]{1,0:T(1,128)} %bitcast.17, bf16[192,128]{1,0:T(8,128)(2,1)} %bitcast.15, bf16[192,128]{1,0:T(8,128)(2,1)} %bitcast.16, bf16[48,768]{1,0:T(8,128)(2,1)} %gate_in.1, ...), custom_call_target="tpu_custom_call" | custom-call | tf_op jit(solution)/shard_map/pallas_call | solution.py:467
  77.6 1.5 %fusion.1 = (bf16[128,192]{0,1:T(8,128)(2,1)}, bf16[128,192]{0,1:T(8,128)(2,1)}) fusion(bf16[2,192,128]{2,1,0:T(8,128)(2,1)} %get-tuple-element.5, bf16[2,192,128]{2,1,0:T(8,128)(2,1)} %get-tuple-element.4), kind=kLoop, calls=%fused_computation.3 | loop fusion | flops 196608 | bytes 294912 | tf_op jit(solution)/shard_map/transpose | solution.py:509
